TPU v7x, 32 devices: a whole 2x2x4 slice. The times are simulated.
32 devices in a mesh: row: 4 (over y, core), col: 8 (over z, x).
Axes of the slice: x: 2, y: 2, z: 4, core: 2. Of those that a mesh axis runs over, the one named last changes fastest.
Arguments:
- object_field: float32 [2, 1024, 2048], P(None, 'row', 'col'), may hold values from -4 to 4
- modes: bfloat16 [4, 12, 2, 256, 256], P('row', None, None, 'col'), may hold values from -5 to 5
- coeffs: float32 [4, 8, 4, 12], P('row', 'col'), may hold values from -1.5 to 1.5
- offsets: int32 [4, 8, 4, 2], P('row', 'col'), may hold values from -128 to 128, as said below
- region: int32 [4, 8, 4], P('row', 'col'), may hold values from 0 to 3, as said below
- counts: int32 [4, 8], P('row', 'col'), may hold values from 1 to 4, as said below
- intensity: bfloat16 [4, 8, 4, 256, 256], P('row', 'col'), may hold values from 0.049804688 to 4
Outputs:
- object_grad: float32 [2, 1024, 2048], P(None, 'row', 'col')
- mode_grad: float32 [4, 12, 2, 256, 256], P('row', None, None, 'col')
Inputs may be any that keep to these rules, and one draw needn't show every extreme that they name: `offsets`: every window reaches at most 128 cells beyond its tile on each side; every tile has a live slot whose window starts at row offset -128 and column offset 256 - 256 / 2. A position's region is its tile's row index or the next one; slot 0 of every tile has its own row's region. Slots 0 to counts - 1 of a tile are live, the rest are ignored; some tile is full and some tile has one live slot.
All inputs are finite; a program needn't handle non-finite values.
Results may differ from a plain program's by a relative error of at most 0.014.
Values may be sent and summed in bfloat16 or wider, within the bound.
No kernel may reach another device: no remote copies, remote signals or barrier semaphores. Data moves between devices by JAX's collectives and lax.ppermute only.
A program may use at most 64 MiB of HBM per device.

v0:
```python
import math
import jax
import jax.numpy as jnp
from jax import lax
from jax.sharding import PartitionSpec as P

FLOOR = 0.25


def extended_2(x, sides, width):
    for axis, dim in sides:
        size, length = (lax.axis_size(axis), x.shape[dim])
        up = [(i, (i + 1) % size) for i in range(size - 1)]
        down = [(j, i) for i, j in up]
        last = lax.slice_in_dim(x, length - width, length, axis=dim)
        leading = lax.slice_in_dim(x, 0, width, axis=dim)
        before = lax.ppermute(last, axis, up)
        after = lax.ppermute(leading, axis, down)
        x = jnp.concatenate([before, x, after], axis=dim)
    return x


def from_behind(value, axis, steps):
    count = lax.axis_size(axis)
    leading, last = (max(0, -steps), min(count, count - steps))
    return lax.ppermute(value, axis, [(source, source + steps) for source in range(leading, last)])


def dft_tables(length):
    indices = jnp.arange(length, dtype=jnp.int32)
    phases = indices[:, None] * indices[None, :] % length
    angles = phases.astype(jnp.float32) * (2.0 * math.pi / length)
    scaling = 1.0 / math.sqrt(length)
    return (
        (jnp.cos(angles) * scaling).astype(jnp.bfloat16),
        (-jnp.sin(angles) * scaling).astype(jnp.bfloat16),
    )


def left_apply(table_re, table_im, real_part, imag_part, orient):

    def multiply(table, operand):
        return jnp.einsum("mr,prn->pmn", table, operand, preferred_element_type=jnp.float32)

    out_re = multiply(table_re, real_part) - orient * multiply(table_im, imag_part)
    out_im = multiply(table_re, imag_part) + orient * multiply(table_im, real_part)
    return (out_re, out_im)


def right_apply(table_re, table_im, real_part, imag_part, orient):

    def multiply(operand, table):
        return jnp.einsum("pmc,cn->pmn", operand, table, preferred_element_type=jnp.float32)

    out_re = multiply(real_part, table_re) - orient * multiply(imag_part, table_im)
    out_im = multiply(imag_part, table_re) + orient * multiply(real_part, table_im)
    return (out_re, out_im)


def local(object_field, modes, coeffs, offsets, region, counts, intensity):
    window_size = modes.shape[-1]
    half_size = window_size // 2
    num_modes = modes.shape[1]
    slot_count = coeffs.shape[2]
    row_index = lax.axis_index("row")
    object_low = object_field.astype(jnp.bfloat16)
    extended = extended_2(object_low, (("row", 1), ("col", 2)), half_size)
    follower = from_behind(modes, "row", -1)
    stacked = jnp.concatenate([modes[0], follower[0]], axis=0)
    stack_count = stacked.shape[0]
    weights = coeffs[0, 0]
    regions = region[0, 0]
    own_mask = (regions == row_index).astype(jnp.float32)
    next_mask = (regions == row_index + 1).astype(jnp.float32)
    mixing = jnp.concatenate([weights * own_mask[:, None], weights * next_mask[:, None]], axis=1)
    mixing_all = lax.all_gather(mixing, "col", axis=0, tiled=True)
    flattened = stacked.reshape(stack_count, -1).astype(jnp.float32)
    slabs = jnp.dot(
        mixing_all, flattened, precision=lax.Precision.HIGHEST, preferred_element_type=jnp.float32
    )
    slabs = slabs.reshape(mixing_all.shape[0], 2, stacked.shape[2], stacked.shape[3]).astype(
        jnp.bfloat16
    )
    probes = lax.all_to_all(slabs, "col", split_axis=0, concat_axis=2, tiled=True)
    corners = offsets[0, 0]

    def cut_window(corner):
        return lax.dynamic_slice(
            extended,
            (jnp.int32(0), corner[0] + half_size, corner[1] + half_size),
            (2, window_size, window_size),
        )

    windows = jax.vmap(cut_window)(corners)
    probe_re = probes[:, 0].astype(jnp.float32)
    probe_im = probes[:, 1].astype(jnp.float32)
    window_re = windows[:, 0].astype(jnp.float32)
    window_im = windows[:, 1].astype(jnp.float32)
    exit_re = (probe_re * window_re - probe_im * window_im).astype(jnp.bfloat16)
    exit_im = (probe_re * window_im + probe_im * window_re).astype(jnp.bfloat16)
    table_re, table_im = dft_tables(window_size)
    half_re, half_im = left_apply(table_re, table_im, exit_re, exit_im, 1.0)
    far_re, far_im = right_apply(
        table_re, table_im, half_re.astype(jnp.bfloat16), half_im.astype(jnp.bfloat16), 1.0
    )
    magnitude = jnp.sqrt(far_re * far_re + far_im * far_im)
    measured = jnp.sqrt(intensity[0, 0].astype(jnp.float32))
    live = (jnp.arange(slot_count, dtype=jnp.int32) < counts[0, 0]).astype(jnp.float32)
    factor = (measured / jnp.maximum(magnitude, FLOOR) - 1.0) * live[:, None, None]
    change_re = (far_re * factor).astype(jnp.bfloat16)
    change_im = (far_im * factor).astype(jnp.bfloat16)
    back_re, back_im = left_apply(table_re, table_im, change_re, change_im, -1.0)
    update_re, update_im = right_apply(
        table_re, table_im, back_re.astype(jnp.bfloat16), back_im.astype(jnp.bfloat16), -1.0
    )
    object_terms = jnp.stack(
        [probe_re * update_re + probe_im * update_im, probe_re * update_im - probe_im * update_re],
        axis=1,
    )
    terms = jnp.stack(
        [
            window_re * update_re + window_im * update_im,
            window_re * update_im - window_im * update_re,
        ],
        axis=1,
    ).astype(jnp.bfloat16)

    def place(position, accum):
        start_row = corners[position, 0] + half_size
        start_col = corners[position, 1] + half_size
        current = lax.dynamic_slice(
            accum, (jnp.int32(0), start_row, start_col), (2, window_size, window_size)
        )
        return lax.dynamic_update_slice(
            accum, current + object_terms[position], (jnp.int32(0), start_row, start_col)
        )

    accum = lax.fori_loop(0, slot_count, place, jnp.zeros(extended.shape, jnp.float32))
    received = lax.all_to_all(terms, "col", split_axis=2, concat_axis=0, tiled=True)
    col_count = lax.axis_size("col")
    per_source = jnp.einsum(
        "dpk,dpx->dkx",
        mixing_all.reshape(col_count, slot_count, -1),
        received.reshape(col_count, slot_count, -1).astype(jnp.float32),
        precision=lax.Precision.HIGHEST,
        preferred_element_type=jnp.float32,
    )
    rounded = lax.optimization_barrier(per_source.astype(jnp.bfloat16)).astype(jnp.float32)
    summed = jnp.sum(rounded, axis=0).reshape(stack_count, 2, received.shape[2], window_size)
    own_sum = summed[:num_modes]
    passed = from_behind(summed[num_modes:].astype(jnp.bfloat16), "row", 1).astype(jnp.float32)
    mode_grad = (own_sum + passed)[None]
    outer_rows = jnp.concatenate([accum[:, :half_size], accum[:, -half_size:]], axis=1)
    got_rows = extended_2(outer_rows.astype(jnp.bfloat16), (("row", 1),), half_size).astype(
        outer_rows.dtype
    )
    middle = accum[:, half_size:-half_size]
    middle = middle.at[:, :half_size].add(got_rows[:, :half_size])
    middle = middle.at[:, -half_size:].add(got_rows[:, -half_size:])
    outer_cols = jnp.concatenate([middle[:, :, :half_size], middle[:, :, -half_size:]], axis=2)
    got_cols = extended_2(outer_cols.astype(jnp.bfloat16), (("col", 2),), half_size).astype(
        outer_cols.dtype
    )
    object_grad = middle[:, :, half_size:-half_size]
    object_grad = object_grad.at[:, :, :half_size].add(got_cols[:, :, :half_size])
    object_grad = object_grad.at[:, :, -half_size:].add(got_cols[:, :, -half_size:])
    return (object_grad, mode_grad)


def solution(mesh):
    in_specs = (
        P(None, "row", "col"),
        P("row", None, None, "col", None),
        P("row", "col", None, None),
        P("row", "col", None, None),
        P("row", "col", None),
        P("row", "col"),
        P("row", "col", None, None, None),
    )
    out_specs = (P(None, "row", "col"), P("row", None, None, "col", None))
    return jax.shard_map(local, mesh=mesh, in_specs=in_specs, out_specs=out_specs, check_vma=False)
```

profile of v0, /device:TPU:30, one launch (start us, length us, event | category | flops | bytes accessed | tf_op | source)
XLA Modules:
  0.0 194.7 jit_solution(16721502046755920107)
XLA Ops:
  1.7 1.9 collective-permute-start.1
  3.7 3.6 %collective-permute-start.2 = (bf16[2,128,256]{2,1,0:T(8,128)(2,1)S(1)}, bf16[2,128,256]{2,1,0:T(8,128)(2,1)S(1)}, u32[]{:S(2)}, u32[]{:S(2)}) collective-permute-start(bf16[2,128,256]{2,1,0:T(8,128)(2,1)S(1)} %get-tuple-element.244), channel_id=1, source_target_pairs={{8,0},{16,8},{24,16},{9,1},{17,9},{25,17},{10,2},{18,10},{26,18},{... | collective-permute-start | bytes 393224 | tf_op jit(solution)/shard_map/ppermute | solution.py:18
  7.3 1.9 collective-permute-start
  10.7 1.3 concatenate.41
  12.0 24.6 %all-gather = f32[8,4,24]{2,1,0:T(4,128)S(1)} all-gather(f32[1,4,24]{2,1,0:T(4,128)S(1)} %maximum_bitcast_fusion), channel_id=1, replica_groups=mesh['row'=4,'col'=8] {'col'}, dimensions={0}, use_global_device_ids=true | all-gather | bytes 3456 | tf_op jit(solution)/shard_map/all_gather | solution.py:76
  36.8 1.3 collective-permute-start.3
  38.1 5.3 %collective-permute-start.4 = (bf16[2,512,128]{2,1,0:T(8,128)(2,1)S(1)}, bf16[2,512,128]{2,1,0:T(8,128)(2,1)}, u32[]{:S(2)}, u32[]{:S(2)}) collective-permute-start(bf16[2,512,128]{2,1,0:T(8,128)(2,1)S(1)} %get-tuple-element.242), channel_id=1, source_target_pairs={{1,0},{2,1},{3,2},{4,3},{5,4},{6,5},{7,6},{9,8},{10,9},{11,10},{12... | collective-permute-start | bytes 786440 | tf_op jit(solution)/shard_map/ppermute | solution.py:18
  45.3 1.6 copy.58
  46.8 6.0 %all-to-all-start = ((bf16[32,2,32,256]{3,2,1,0:T(8,128)(2,1)}), bf16[32,2,32,256]{3,2,1,0:T(8,128)(2,1)S(1)}, u32[]{:S(2)}, u32[]{:S(2)}) async-start(bf16[32,2,32,256]{3,2,1,0:T(8,128)(2,1)} %copy.58), calls=%async_computation | async-start | bytes 2097152 | tf_op jit(solution)/shard_map/all_to_all | solution.py:84
  56.7 11.2 %while.22 = (s32[]{:T(128)}, bf16[2,512,512]{2,1,0:T(8,128)(2,1)S(1)}, s32[4,3]{1,0:T(4,128)}, bf16[4,2,256,256]{3,2,0,1:T(8,128)(2,1)S(1)}, s32[]{:T(128)}) while((s32[]{:T(128)}, bf16[2,512,512]{2,1,0:T(8,128)(2,1)S(1)}, s32[4,3]{1,0:T(4,128)}, bf16[4,2,256,256]{3,2,0,1:T(8,128)(2,1)S(1)}, s32[]{:T(128)}) %tuple.95), condition=%wide.while_cond.4, body=%wide.while_body.4.sunk | while | flops 2 | bytes 524413 | solution.py:88
  58.0 1.5 bitcast_dynamic-update-slice_fusion.2
  60.7 1.5 bitcast_dynamic-update-slice_fusion.2
  63.5 1.5 bitcast_dynamic-update-slice_fusion.2
  66.3 1.5 bitcast_dynamic-update-slice_fusion.2
  67.9 4.4 %all-to-all-done = bf16[32,2,32,256]{3,2,1,0:T(8,128)(2,1)S(1)} async-done(((bf16[32,2,32,256]{3,2,1,0:T(8,128)(2,1)}), bf16[32,2,32,256]{3,2,1,0:T(8,128)(2,1)S(1)}, u32[]{:S(2)}, u32[]{:S(2)}) %all-to-all-start) | async-done | bytes 1048608 | tf_op jit(solution)/shard_map/all_to_all | solution.py:84
  75.4 1.3 fusion.9
  76.6 1.3 fusion.8
  77.9 1.3 fusion.57
  80.4 1.3 convolution_add_fusion
  81.7 2.0 %multiply_convert_fusion.1 = (bf16[4,256,256]{2,1,0:T(8,128)(2,1)S(1)}, bf16[4,256,256]{2,1,0:T(8,128)(2,1)S(1)}) fusion(f32[4]{0:T(128)S(1)} %copy-done.7, f32[4,256,256]{2,1,0:T(8,128)S(1)} %convolution_add_fusion, bf16[1,1,4,256,256]{4,3,2,1,0:T(8,128)(2,1)S(1)} %copy-done.6, f32[4,256,256]{2,1,0:T(8,128)S(1)} %fusion.61, bf16[4,256,256]{1,2,0:T(8,128)(2,1)S(1)} %fusion.8), kind=kOutput, calls=%fused_computation.61 | convolution fusion | flops 138739712 | bytes 4194320 | tf_op jit(solution)/shard_map/pmc,cn->pmn/dot_general | solution.py:53
  83.7 1.5 fusion.55
  86.5 1.3 fusion.11
  87.7 1.3 fusion.10
  90.2 1.3 fusion.53
  91.5 1.3 fusion
  92.8 1.8 fusion.28
  94.7 1.8 copy.80
  96.5 6.7 %all-to-all-start.1 = ((bf16[4,2,256,256]{3,0,1,2:T(4,128)(2,1)}), bf16[4,2,256,256]{3,0,1,2:T(4,128)(2,1)}, u32[]{:S(2)}, u32[]{:S(2)}) async-start(bf16[4,2,256,256]{3,0,1,2:T(4,128)(2,1)} %copy.80), calls=%async_computation.1 | async-start | bytes 2097152 | tf_op jit(solution)/shard_map/all_to_all | solution.py:139
  103.2 1.6 pad_maximum_fusion
  105.5 53.2 %while.21 = (s32[]{:T(128)}, f32[2,512,512]{2,1,0:T(8,128)S(1)}, s32[4,2]{0,1:T(2,128)S(1)}, f32[4,2,256,256]{3,2,0,1:T(8,128)}, s32[]{:T(128)}, /*index=5*/s32[1,1]{0,1:T(1,128)}, s32[]{:T(128)}, s32[1,1]{0,1:T(1,128)}) while((s32[]{:T(128)}, f32[2,512,512]{2,1,0:T(8,128)S(1)}, s32[4,2]{0,1:T(2,128)S(1)}, f32[4,2,256,256]{3,2,0,1:T(8,128)}, ...), condition=%wide.region_1.2_spmd, body=%wide.region_0.1_spmd.sunk | while | flops 131082 | bytes 2621661 | solution.py:138
  108.7 1.3 bitcast_add_fusion.2
  109.9 6.0 %dynamic_update_slice.12 = f32[2,512,512]{2,1,0:T(8,128)S(1)} dynamic-update-slice(f32[2,512,512]{2,1,0:T(8,128)S(1)} %get-tuple-element.333, f32[2,256,256]{2,1,0:T(8,128)S(1)} %bitcast_add_fusion.2, s32[]{:T(128)} %constant.199.clone.1..sunk, s32[]{:T(128)S(6)} %select_n.116, s32[]{:T(128)S(6)} %select_n.117) | dynamic-update-slice | bytes 1048580 | tf_op jit(solution)/shard_map/while/body/eval_jaxpr/dynamic_update_slice | solution.py:134
  119.1 1.3 bitcast_add_fusion.2
  120.4 8.7 %dynamic_update_slice.12 = f32[2,512,512]{2,1,0:T(8,128)S(1)} dynamic-update-slice(f32[2,512,512]{2,1,0:T(8,128)S(1)} %get-tuple-element.333, f32[2,256,256]{2,1,0:T(8,128)S(1)} %bitcast_add_fusion.2, s32[]{:T(128)} %constant.199.clone.1..sunk, s32[]{:T(128)S(6)} %select_n.116, s32[]{:T(128)S(6)} %select_n.117) | dynamic-update-slice | bytes 1048580 | tf_op jit(solution)/shard_map/while/body/eval_jaxpr/dynamic_update_slice | solution.py:134
  132.3 1.3 bitcast_add_fusion.2
  133.6 10.2 %dynamic_update_slice.12 = f32[2,512,512]{2,1,0:T(8,128)S(1)} dynamic-update-slice(f32[2,512,512]{2,1,0:T(8,128)S(1)} %get-tuple-element.333, f32[2,256,256]{2,1,0:T(8,128)S(1)} %bitcast_add_fusion.2, s32[]{:T(128)} %constant.199.clone.1..sunk, s32[]{:T(128)S(6)} %select_n.116, s32[]{:T(128)S(6)} %select_n.117) | dynamic-update-slice | bytes 1048580 | tf_op jit(solution)/shard_map/while/body/eval_jaxpr/dynamic_update_slice | solution.py:134
  147.0 1.3 bitcast_add_fusion.2
  148.3 10.4 %dynamic_update_slice.12 = f32[2,512,512]{2,1,0:T(8,128)S(1)} dynamic-update-slice(f32[2,512,512]{2,1,0:T(8,128)S(1)} %get-tuple-element.333, f32[2,256,256]{2,1,0:T(8,128)S(1)} %bitcast_add_fusion.2, s32[]{:T(128)} %constant.199.clone.1..sunk, s32[]{:T(128)S(6)} %select_n.116, s32[]{:T(128)S(6)} %select_n.117) | dynamic-update-slice | bytes 1048580 | tf_op jit(solution)/shard_map/while/body/eval_jaxpr/dynamic_update_slice | solution.py:134
  158.9 2.2 %collective-permute-start.5 = (bf16[2,128,512]{2,1,0:T(8,128)(2,1)S(1)}, bf16[2,128,512]{2,1,0:T(8,128)(2,1)S(1)}, u32[]{:S(2)}, u32[]{:S(2)}) collective-permute-start(bf16[2,128,512]{2,1,0:T(8,128)(2,1)S(1)} %get-tuple-element.237), channel_id=1, source_target_pairs={{0,8},{8,16},{16,24},{1,9},{9,17},{17,25},{2,10},{10,18},{18,26},{... | collective-permute-start | bytes 786440 | tf_op jit(solution)/shard_map/ppermute | solution.py:17
  161.1 3.6 %collective-permute-start.6 = (bf16[2,128,512]{2,1,0:T(8,128)(2,1)S(1)}, bf16[2,128,512]{2,1,0:T(8,128)(2,1)S(1)}, u32[]{:S(2)}, u32[]{:S(2)}) collective-permute-start(bf16[2,128,512]{2,1,0:T(8,128)(2,1)S(1)} %get-tuple-element.238), channel_id=1, source_target_pairs={{8,0},{16,8},{24,16},{9,1},{17,9},{25,17},{10,2},{18,10},{26,18},{... | collective-permute-start | bytes 786440 | tf_op jit(solution)/shard_map/ppermute | solution.py:18
  164.8 1.8 collective-permute-done.5
  166.6 2.0 %collective-permute-done.6 = bf16[2,128,512]{2,1,0:T(8,128)(2,1)S(1)} collective-permute-done((bf16[2,128,512]{2,1,0:T(8,128)(2,1)S(1)}, bf16[2,128,512]{2,1,0:T(8,128)(2,1)S(1)}, u32[]{:S(2)}, u32[]{:S(2)}) %collective-permute-start.6) | collective-permute-done | bytes 262176 | tf_op jit(solution)/shard_map/ppermute | solution.py:18
  169.9 1.3 collective-permute-start.7
  171.2 4.6 %collective-permute-start.8 = (bf16[2,256,128]{2,1,0:T(8,128)(2,1)S(1)}, bf16[2,256,128]{2,1,0:T(8,128)(2,1)S(1)}, u32[]{:S(2)}, u32[]{:S(2)}) collective-permute-start(bf16[2,256,128]{2,1,0:T(8,128)(2,1)S(1)} %get-tuple-element.240), channel_id=1, source_target_pairs={{1,0},{2,1},{3,2},{4,3},{5,4},{6,5},{7,6},{9,8},{10,9},{11,10},{12... | collective-permute-start | bytes 393224 | tf_op jit(solution)/shard_map/ppermute | solution.py:18
  175.7 1.5 copy.109
  178.0 5.5 %convolution_convert_fusion = bf16[8,24,16384]{2,1,0:T(8,128)(2,1)S(1)} fusion(f32[8,4,24]{2,1,0:T(4,128)S(1)} %all-gather, bf16[8,4,16384]{2,1,0:T(4,128)(2,1)S(1)} %reshape.183), kind=kOutput, calls=%fused_computation.5 | convolution fusion | flops 154140672 | bytes 7343104 | tf_op jit(solution)/shard_map/dpk,dpx->dkx/dot_general | solution.py:141
  184.6 1.9 collective-permute-start.9
  188.5 5.3 %collective-permute-done.9 = bf16[12,2,32,256]{3,2,1,0:T(8,128)(2,1)S(1)} collective-permute-done((bf16[12,2,32,256]{3,2,1,0:T(8,128)(2,1)S(1)}, bf16[12,2,32,256]{3,2,1,0:T(8,128)(2,1)S(1)}, u32[]{:S(2)}, u32[]{:S(2)}) %collective-permute-start.9) | collective-permute-done | bytes 393248 | tf_op jit(solution)/shard_map/ppermute | solution.py:26
  (82 shorter events, 29.0 us)
Async XLA Ops:
  1.7 34.9 %collective-permute-start.1 = (bf16[2,128,256]{2,1,0:T(8,128)(2,1)S(1)}, bf16[2,128,256]{2,1,0:T(8,128)(2,1)S(1)}, u32[]{:S(2)}, u32[]{:S(2)}) collective-permute-start(bf16[2,128,256]{2,1,0:T(8,128)(2,1)S(1)} %get-tuple-element.243), channel_id=1, source_target_pairs={{0,8},{8,16},{16,24},{1,9},{9,17},{17,25},{2,10},{10,18},{18,26},{... | collective-permute-start | bytes 393224 | tf_op jit(solution)/shard_map/ppermute | solution.py:17
  3.7 33.0 %collective-permute-start.2 = (bf16[2,128,256]{2,1,0:T(8,128)(2,1)S(1)}, bf16[2,128,256]{2,1,0:T(8,128)(2,1)S(1)}, u32[]{:S(2)}, u32[]{:S(2)}) collective-permute-start(bf16[2,128,256]{2,1,0:T(8,128)(2,1)S(1)} %get-tuple-element.244), channel_id=1, source_target_pairs={{8,0},{16,8},{24,16},{9,1},{17,9},{25,17},{10,2},{18,10},{26,18},{... | collective-permute-start | bytes 393224 | tf_op jit(solution)/shard_map/ppermute | solution.py:18
  7.3 36.0 %collective-permute-start = (bf16[1,12,2,32,256]{4,3,2,1,0:T(8,128)(2,1)}, bf16[1,12,2,32,256]{4,3,2,1,0:T(8,128)(2,1)S(1)}, u32[]{:S(2)}, u32[]{:S(2)}) collective-permute-start(bf16[1,12,2,32,256]{4,3,2,1,0:T(8,128)(2,1)} %param.18), channel_id=1, source_target_pairs={{8,0},{16,8},{24,16},{9,1},{17,9},{25,17},{10,2},{18,10},{26,18},{... | collective-permute-start | bytes 1179656 | tf_op jit(solution)/shard_map/ppermute | solution.py:26
  36.6 7.2 %copy-start.2 = (bf16[2,128,256]{2,1,0:T(8,128)(2,1)}, bf16[2,128,256]{2,1,0:T(8,128)(2,1)S(1)}, u32[]{:S(2)}) copy-start(bf16[2,128,256]{2,1,0:T(8,128)(2,1)S(1)} %collective-permute-done.2) | copy-start | bytes 393220
  36.8 18.0 %collective-permute-start.3 = (bf16[2,512,128]{2,1,0:T(8,128)(2,1)S(1)}, bf16[2,512,128]{2,1,0:T(8,128)(2,1)S(1)}, u32[]{:S(2)}, u32[]{:S(2)}) collective-permute-start(bf16[2,512,128]{2,1,0:T(8,128)(2,1)S(1)} %get-tuple-element.241), channel_id=1, source_target_pairs={{0,1},{1,2},{2,3},{3,4},{4,5},{5,6},{6,7},{8,9},{9,10},{10,11},{11... | collective-permute-start | bytes 786440 | tf_op jit(solution)/shard_map/ppermute | solution.py:17
  38.1 17.4 %collective-permute-start.4 = (bf16[2,512,128]{2,1,0:T(8,128)(2,1)S(1)}, bf16[2,512,128]{2,1,0:T(8,128)(2,1)}, u32[]{:S(2)}, u32[]{:S(2)}) collective-permute-start(bf16[2,512,128]{2,1,0:T(8,128)(2,1)S(1)} %get-tuple-element.242), channel_id=1, source_target_pairs={{1,0},{2,1},{3,2},{4,3},{5,4},{6,5},{7,6},{9,8},{10,9},{11,10},{12... | collective-permute-start | bytes 786440 | tf_op jit(solution)/shard_map/ppermute | solution.py:18
  45.3 7.6 %copy-start.4 = (s32[1,1,4,2]{2,3,1,0:T(2,128)S(1)}, s32[1,1,4,2]{2,3,1,0:T(2,128)}, u32[]{:S(2)}) copy-start(s32[1,1,4,2]{2,3,1,0:T(2,128)} %param.20) | copy-start | bytes 100
  46.8 25.5 %all-to-all-start = ((bf16[32,2,32,256]{3,2,1,0:T(8,128)(2,1)}), bf16[32,2,32,256]{3,2,1,0:T(8,128)(2,1)S(1)}, u32[]{:S(2)}, u32[]{:S(2)}) async-start(bf16[32,2,32,256]{3,2,1,0:T(8,128)(2,1)} %copy.58), calls=%async_computation | async-start | bytes 2097152 | tf_op jit(solution)/shard_map/all_to_all | solution.py:84
  54.8 0.7 copy-start.3
  79.1 2.5 %copy-start.6 = (bf16[1,1,4,256,256]{4,3,2,1,0:T(8,128)(2,1)S(1)}, bf16[1,1,4,256,256]{4,3,2,1,0:T(8,128)(2,1)}, u32[]{:S(2)}) copy-start(bf16[1,1,4,256,256]{4,3,2,1,0:T(8,128)(2,1)} %param.23) | copy-start | bytes 1572868
  79.1 2.5 %copy-start.7 = (f32[4]{0:T(128)S(1)}, f32[4]{0:T(128)}, u32[]{:S(2)}) copy-start(f32[4]{0:T(128)} %compare_convert_fusion) | copy-start | bytes 52
  96.5 79.3 %all-to-all-start.1 = ((bf16[4,2,256,256]{3,0,1,2:T(4,128)(2,1)}), bf16[4,2,256,256]{3,0,1,2:T(4,128)(2,1)}, u32[]{:S(2)}, u32[]{:S(2)}) async-start(bf16[4,2,256,256]{3,0,1,2:T(4,128)(2,1)} %copy.80), calls=%async_computation.1 | async-start | bytes 2097152 | tf_op jit(solution)/shard_map/all_to_all | solution.py:139
  104.8 0.7 copy-start.5
  158.9 7.7 %collective-permute-start.5 = (bf16[2,128,512]{2,1,0:T(8,128)(2,1)S(1)}, bf16[2,128,512]{2,1,0:T(8,128)(2,1)S(1)}, u32[]{:S(2)}, u32[]{:S(2)}) collective-permute-start(bf16[2,128,512]{2,1,0:T(8,128)(2,1)S(1)} %get-tuple-element.237), channel_id=1, source_target_pairs={{0,8},{8,16},{16,24},{1,9},{9,17},{17,25},{2,10},{10,18},{18,26},{... | collective-permute-start | bytes 786440 | tf_op jit(solution)/shard_map/ppermute | solution.py:17
  161.1 7.5 %collective-permute-start.6 = (bf16[2,128,512]{2,1,0:T(8,128)(2,1)S(1)}, bf16[2,128,512]{2,1,0:T(8,128)(2,1)S(1)}, u32[]{:S(2)}, u32[]{:S(2)}) collective-permute-start(bf16[2,128,512]{2,1,0:T(8,128)(2,1)S(1)} %get-tuple-element.238), channel_id=1, source_target_pairs={{8,0},{16,8},{24,16},{9,1},{17,9},{25,17},{10,2},{18,10},{26,18},{... | collective-permute-start | bytes 786440 | tf_op jit(solution)/shard_map/ppermute | solution.py:18
  168.8 1.0 copy-start
  169.9 16.7 %collective-permute-start.7 = (bf16[2,256,128]{2,1,0:T(8,128)(2,1)S(1)}, bf16[2,256,128]{2,1,0:T(8,128)(2,1)S(1)}, u32[]{:S(2)}, u32[]{:S(2)}) collective-permute-start(bf16[2,256,128]{2,1,0:T(8,128)(2,1)S(1)} %get-tuple-element.239), channel_id=1, source_target_pairs={{0,1},{1,2},{2,3},{3,4},{4,5},{5,6},{6,7},{8,9},{9,10},{10,11},{11... | collective-permute-start | bytes 393224 | tf_op jit(solution)/shard_map/ppermute | solution.py:17
  171.2 15.4 %collective-permute-start.8 = (bf16[2,256,128]{2,1,0:T(8,128)(2,1)S(1)}, bf16[2,256,128]{2,1,0:T(8,128)(2,1)S(1)}, u32[]{:S(2)}, u32[]{:S(2)}) collective-permute-start(bf16[2,256,128]{2,1,0:T(8,128)(2,1)S(1)} %get-tuple-element.240), channel_id=1, source_target_pairs={{1,0},{2,1},{3,2},{4,3},{5,4},{6,5},{7,6},{9,8},{10,9},{11,10},{12... | collective-permute-start | bytes 393224 | tf_op jit(solution)/shard_map/ppermute | solution.py:18
  184.6 9.1 %collective-permute-start.9 = (bf16[12,2,32,256]{3,2,1,0:T(8,128)(2,1)S(1)}, bf16[12,2,32,256]{3,2,1,0:T(8,128)(2,1)S(1)}, u32[]{:S(2)}, u32[]{:S(2)}) collective-permute-start(bf16[12,2,32,256]{3,2,1,0:T(8,128)(2,1)S(1)} %bitcast.189), channel_id=1, source_target_pairs={{0,8},{8,16},{16,24},{1,9},{9,17},{17,25},{2,10},{10,18},{18,26},{... | collective-permute-start | bytes 1179656 | tf_op jit(solution)/shard_map/ppermute | solution.py:26
  187.6 0.8 copy-start.1
where the time goes:
time: 196 us; the launch traced here: 195 us
  local copies, waits for them, and re-layouts  60.4 us (31%)
  starting transfers between devices  40.3 us (21%)
  matrix products  28.3 us (14%)
  blocking collectives  24.6 us (13%)
  other arithmetic  15 us (8%)
  waiting for transfers between devices  13.5 us (7%)
  loops' own time  10.8 us (6%)
    dynamic_update_slice x4, local copies, waits for them, and re-layouts, place(): lax.dynamic_update_slice(accum, current + object_terms[position], (jnp.in...  35.3 us
    all_gather x1, blocking collectives, local(): mixing_all = lax.all_gather(mixing, 'col', axis=0, tiled=True)  24.6 us
    ppermute x4, starting transfers between devices, extended_2(): after = lax.ppermute(leading, axis, down)  17.1 us
    dot_general x8, matrix products, multiply(): jnp.einsum('pmc,cn->pmn', operand, table, preferred_element_type=jnp.floa...  11.4 us
    gather x12, local copies, waits for them, and re-layouts  11 us
    another operation x1, loops' own time, local(): lax.fori_loop(0, slot_count, place, jnp.zeros(extended.shape, jnp.float32))  10.5 us
    dot_general x8, matrix products, multiply(): jnp.einsum('mr,prn->pmn', table, operand, preferred_element_type=jnp.floa...  10.2 us
    all_to_all x1, starting transfers between devices, local(): lax.all_to_all(terms, 'col', split_axis=2, concat_axis=0, tiled=True)  6.72 us
  transfers between devices with their start and end apart: 12, of which 4 were waited for; matrix products, arithmetic and copies ran while one was open for 39% of the time, Pallas kernels for 0%

commit v1 on v0

--- a/solution.py
+++ b/solution.py
@@ -73,7 +73,12 @@
     own_mask = (regions == row_index).astype(jnp.float32)
     next_mask = (regions == row_index + 1).astype(jnp.float32)
     mixing = jnp.concatenate([weights * own_mask[:, None], weights * next_mask[:, None]], axis=1)
-    mixing_all = lax.all_gather(mixing, "col", axis=0, tiled=True)
+    ring = [mixing]
+    for hop in range(7):
+        ring.append(lax.ppermute(ring[-1], "col", [(dev, (dev + 1) % 8) for dev in range(8)]))
+    mixing_all = jnp.roll(
+        jnp.concatenate(ring[::-1], axis=0), (lax.axis_index("col") + 1) * ring[0].shape[0], axis=0
+    )
     flattened = stacked.reshape(stack_count, -1).astype(jnp.float32)
     slabs = jnp.dot(
         mixing_all, flattened, precision=lax.Precision.HIGHEST, preferred_element_type=jnp.float32

time: 196 us -> 205 us (1.046)
  starting transfers between devices: 40.3 us -> 67.8 us
  blocking collectives: 24.6 us -> 0 us
  waiting for transfers between devices: 13.5 us -> 20 us
    ppermute x0 -> x7, starting transfers between devices: none -> 27.5 us  [local(): lax.ppermute(ring[-1], 'col', [(dev, (dev + 1) % 8) for dev in range(8)])]
    all_gather x1 -> x0, blocking collectives: 24.6 us -> none  [local(): mixing_all = lax.all_gather(mixing, 'col', axis=0, tiled=True)]
    ppermute x0 -> x7, waiting for transfers between devices: none -> 9.26 us  [local(): lax.ppermute(ring[-1], 'col', [(dev, (dev + 1) % 8) for dev in range(8)])]
    all_to_all x1, waiting for transfers between devices: 4.41 us -> 1.71 us  [local(): lax.all_to_all(slabs, 'col', split_axis=0, concat_axis=2, tiled=True)]
  transfers between devices with their start and end apart: 12 -> 19, of which waited for: 4 -> 10; matrix products, arithmetic and copies ran while one was open for 39% -> 37% of each run, Pallas kernels for 0% -> 0%
where the time goes in v1:
time: 205 us; the launch traced here: 203 us
  starting transfers between devices  67.8 us (33%)
  local copies, waits for them, and re-layouts  59.8 us (29%)
  matrix products  28.3 us (14%)
  waiting for transfers between devices  20 us (10%)
  other arithmetic  14.9 us (7%)
  loops' own time  10.8 us (5%)
    dynamic_update_slice x4, local copies, waits for them, and re-layouts, place(): lax.dynamic_update_slice(accum, current + object_terms[position], (jnp.in...  35.3 us
    ppermute x7, starting transfers between devices, local(): lax.ppermute(ring[-1], 'col', [(dev, (dev + 1) % 8) for dev in range(8)])  27.5 us
    ppermute x4, starting transfers between devices, extended_2(): after = lax.ppermute(leading, axis, down)  17.1 us
    dot_general x8, matrix products, multiply(): jnp.einsum('pmc,cn->pmn', operand, table, preferred_element_type=jnp.floa...  11.4 us
    gather x12, local copies, waits for them, and re-layouts  11.2 us
    another operation x1, loops' own time, local(): lax.fori_loop(0, slot_count, place, jnp.zeros(extended.shape, jnp.float32))  10.5 us
    dot_general x8, matrix products, multiply(): jnp.einsum('mr,prn->pmn', table, operand, preferred_element_type=jnp.floa...  10.2 us
    ppermute x7, waiting for transfers between devices, local(): lax.ppermute(ring[-1], 'col', [(dev, (dev + 1) % 8) for dev in range(8)])  9.26 us
  transfers between devices with their start and end apart: 19, of which 10 were waited for; matrix products, arithmetic and copies ran while one was open for 37% of the time, Pallas kernels for 0%

profile of v1, /device:TPU:30, one launch (start us, length us, event | category | flops | bytes accessed | tf_op | source)
XLA Modules:
  0.0 203.5 jit_solution(8888020733432683714)
XLA Ops:
  1.7 1.9 collective-permute-start.8
  3.7 3.6 %collective-permute-start.9 = (bf16[2,128,256]{2,1,0:T(8,128)(2,1)S(1)}, bf16[2,128,256]{2,1,0:T(8,128)(2,1)S(1)}, u32[]{:S(2)}, u32[]{:S(2)}) collective-permute-start(bf16[2,128,256]{2,1,0:T(8,128)(2,1)S(1)} %get-tuple-element.244), channel_id=1, source_target_pairs={{8,0},{16,8},{24,16},{9,1},{17,9},{25,17},{10,2},{18,10},{26,18},{... | collective-permute-start | bytes 393224 | tf_op jit(solution)/shard_map/ppermute | solution.py:18
  9.1 3.5 %collective-permute-done = f32[4,24]{0,1:T(8,128)S(1)} collective-permute-done((f32[4,24]{0,1:T(8,128)S(1)}, f32[4,24]{0,1:T(8,128)S(1)}, u32[]{:S(2)}, u32[]{:S(2)}) %collective-permute-start) | collective-permute-done | bytes 416 | tf_op jit(solution)/shard_map/ppermute | solution.py:78
  12.6 2.9 %collective-permute-start.1 = (f32[4,24]{0,1:T(8,128)S(1)}, f32[4,24]{0,1:T(8,128)S(1)}, u32[]{:S(2)}, u32[]{:S(2)}) collective-permute-start(f32[4,24]{0,1:T(8,128)S(1)} %collective-permute-done), channel_id=1, source_target_pairs={{0,1},{1,2},{2,3},{3,4},{4,5},{5,6},{6,7},{7,0},{8,9},{9,10},{10,1... | collective-permute-start | bytes 1160 | tf_op jit(solution)/shard_map/ppermute | solution.py:78
  15.5 1.4 collective-permute-done.1
  16.9 5.0 %collective-permute-start.2 = (f32[4,24]{0,1:T(8,128)S(1)}, f32[4,24]{0,1:T(8,128)S(1)}, u32[]{:S(2)}, u32[]{:S(2)}) collective-permute-start(f32[4,24]{0,1:T(8,128)S(1)} %collective-permute-done.1), channel_id=1, source_target_pairs={{0,1},{1,2},{2,3},{3,4},{4,5},{5,6},{6,7},{7,0},{8,9},{9,10},{10,1... | collective-permute-start | bytes 1160 | tf_op jit(solution)/shard_map/ppermute | solution.py:78
  21.9 1.4 collective-permute-done.2
  23.3 5.0 %collective-permute-start.3 = (f32[4,24]{0,1:T(8,128)S(1)}, f32[4,24]{0,1:T(8,128)S(1)}, u32[]{:S(2)}, u32[]{:S(2)}) collective-permute-start(f32[4,24]{0,1:T(8,128)S(1)} %collective-permute-done.2), channel_id=1, source_target_pairs={{0,1},{1,2},{2,3},{3,4},{4,5},{5,6},{6,7},{7,0},{8,9},{9,10},{10,1... | collective-permute-start | bytes 1160 | tf_op jit(solution)/shard_map/ppermute | solution.py:78
  28.3 1.9 collective-permute-start.7
  30.2 4.5 %collective-permute-start.4 = (f32[4,24]{0,1:T(8,128)S(1)}, f32[4,24]{0,1:T(8,128)S(1)}, u32[]{:S(2)}, u32[]{:S(2)}) collective-permute-start(f32[4,24]{0,1:T(8,128)S(1)} %collective-permute-done.3), channel_id=1, source_target_pairs={{0,1},{1,2},{2,3},{3,4},{4,5},{5,6},{6,7},{7,0},{8,9},{9,10},{10,1... | collective-permute-start | bytes 1160 | tf_op jit(solution)/shard_map/ppermute | solution.py:78
  34.7 1.4 collective-permute-done.4
  36.1 5.0 %collective-permute-start.5 = (f32[4,24]{0,1:T(8,128)S(1)}, f32[4,24]{0,1:T(8,128)S(1)}, u32[]{:S(2)}, u32[]{:S(2)}) collective-permute-start(f32[4,24]{0,1:T(8,128)S(1)} %collective-permute-done.4), channel_id=1, source_target_pairs={{0,1},{1,2},{2,3},{3,4},{4,5},{5,6},{6,7},{7,0},{8,9},{9,10},{10,1... | collective-permute-start | bytes 1160 | tf_op jit(solution)/shard_map/ppermute | solution.py:78
  41.1 1.3 concatenate.48
  42.5 5.0 %collective-permute-start.6 = (f32[4,24]{0,1:T(8,128)S(1)}, f32[4,24]{0,1:T(8,128)S(1)}, u32[]{:S(2)}, u32[]{:S(2)}) collective-permute-start(f32[4,24]{0,1:T(8,128)S(1)} %collective-permute-done.5), channel_id=1, source_target_pairs={{0,1},{1,2},{2,3},{3,4},{4,5},{5,6},{6,7},{7,0},{8,9},{9,10},{10,1... | collective-permute-start | bytes 1160 | tf_op jit(solution)/shard_map/ppermute | solution.py:78
  47.4 1.4 collective-permute-done.6
  49.2 1.3 collective-permute-start.10
  50.5 5.2 %collective-permute-start.11 = (bf16[2,512,128]{2,1,0:T(8,128)(2,1)S(1)}, bf16[2,512,128]{2,1,0:T(8,128)(2,1)}, u32[]{:S(2)}, u32[]{:S(2)}) collective-permute-start(bf16[2,512,128]{2,1,0:T(8,128)(2,1)S(1)} %get-tuple-element.242), channel_id=1, source_target_pairs={{1,0},{2,1},{3,2},{4,3},{5,4},{6,5},{7,6},{9,8},{10,9},{11,10},{12... | collective-permute-start | bytes 786440 | tf_op jit(solution)/shard_map/ppermute | solution.py:18
  57.7 1.6 copy.63
  59.2 6.0 %all-to-all-start = ((bf16[32,2,32,256]{3,2,1,0:T(8,128)(2,1)}), bf16[32,2,32,256]{3,2,1,0:T(8,128)(2,1)S(1)}, u32[]{:S(2)}, u32[]{:S(2)}) async-start(bf16[32,2,32,256]{3,2,1,0:T(8,128)(2,1)} %copy.63), calls=%async_computation | async-start | bytes 2097152 | tf_op jit(solution)/shard_map/all_to_all | solution.py:89
  68.4 11.5 %while.22 = (s32[]{:T(128)}, bf16[2,512,512]{2,1,0:T(8,128)(2,1)S(1)}, s32[4,3]{1,0:T(4,128)}, bf16[4,2,256,256]{3,2,0,1:T(8,128)(2,1)S(1)}, s32[]{:T(128)}) while((s32[]{:T(128)}, bf16[2,512,512]{2,1,0:T(8,128)(2,1)S(1)}, s32[4,3]{1,0:T(4,128)}, bf16[4,2,256,256]{3,2,0,1:T(8,128)(2,1)S(1)}, s32[]{:T(128)}) %tuple.95), condition=%wide.while_cond.4, body=%wide.while_body.4.sunk | while | flops 2 | bytes 524413 | solution.py:93
  69.7 1.5 bitcast_dynamic-update-slice_fusion.2
  72.6 1.5 bitcast_dynamic-update-slice_fusion.2
  75.4 1.5 bitcast_dynamic-update-slice_fusion.2
  78.2 1.5 bitcast_dynamic-update-slice_fusion.2
  79.9 1.7 all-to-all-done
  89.6 1.3 convolution_add_fusion
  90.9 2.0 multiply_convert_fusion.1
  93.0 1.5 fusion.55
  102.0 1.8 fusion.28
  103.9 1.8 copy.86
  105.7 6.7 %all-to-all-start.1 = ((bf16[4,2,256,256]{3,0,1,2:T(4,128)(2,1)}), bf16[4,2,256,256]{3,0,1,2:T(4,128)(2,1)}, u32[]{:S(2)}, u32[]{:S(2)}) async-start(bf16[4,2,256,256]{3,0,1,2:T(4,128)(2,1)} %copy.86), calls=%async_computation.1 | async-start | bytes 2097152 | tf_op jit(solution)/shard_map/all_to_all | solution.py:144
  112.4 1.5 pad_maximum_fusion
  114.2 53.2 %while.21 = (s32[]{:T(128)}, f32[2,512,512]{2,1,0:T(8,128)S(1)}, s32[4,2]{0,1:T(2,128)S(1)}, f32[4,2,256,256]{3,2,0,1:T(8,128)}, s32[]{:T(128)}, /*index=5*/s32[1,1]{0,1:T(1,128)}, s32[]{:T(128)}, s32[1,1]{0,1:T(1,128)}) while((s32[]{:T(128)}, f32[2,512,512]{2,1,0:T(8,128)S(1)}, s32[4,2]{0,1:T(2,128)S(1)}, f32[4,2,256,256]{3,2,0,1:T(8,128)}, ...), condition=%wide.region_1.2_spmd, body=%wide.region_0.1_spmd.sunk | while | flops 131082 | bytes 2621661 | solution.py:143
  117.4 1.3 bitcast_add_fusion.2
  118.7 6.0 %dynamic_update_slice.12 = f32[2,512,512]{2,1,0:T(8,128)S(1)} dynamic-update-slice(f32[2,512,512]{2,1,0:T(8,128)S(1)} %get-tuple-element.333, f32[2,256,256]{2,1,0:T(8,128)S(1)} %bitcast_add_fusion.2, s32[]{:T(128)} %constant.220.clone.1..sunk, s32[]{:T(128)S(6)} %select_n.130, s32[]{:T(128)S(6)} %select_n.131) | dynamic-update-slice | bytes 1048580 | tf_op jit(solution)/shard_map/while/body/eval_jaxpr/dynamic_update_slice | solution.py:139
  129.1 8.7 %dynamic_update_slice.12 = f32[2,512,512]{2,1,0:T(8,128)S(1)} dynamic-update-slice(f32[2,512,512]{2,1,0:T(8,128)S(1)} %get-tuple-element.333, f32[2,256,256]{2,1,0:T(8,128)S(1)} %bitcast_add_fusion.2, s32[]{:T(128)} %constant.220.clone.1..sunk, s32[]{:T(128)S(6)} %select_n.130, s32[]{:T(128)S(6)} %select_n.131) | dynamic-update-slice | bytes 1048580 | tf_op jit(solution)/shard_map/while/body/eval_jaxpr/dynamic_update_slice | solution.py:139
  142.3 10.2 %dynamic_update_slice.12 = f32[2,512,512]{2,1,0:T(8,128)S(1)} dynamic-update-slice(f32[2,512,512]{2,1,0:T(8,128)S(1)} %get-tuple-element.333, f32[2,256,256]{2,1,0:T(8,128)S(1)} %bitcast_add_fusion.2, s32[]{:T(128)} %constant.220.clone.1..sunk, s32[]{:T(128)S(6)} %select_n.130, s32[]{:T(128)S(6)} %select_n.131) | dynamic-update-slice | bytes 1048580 | tf_op jit(solution)/shard_map/while/body/eval_jaxpr/dynamic_update_slice | solution.py:139
  157.0 10.4 %dynamic_update_slice.12 = f32[2,512,512]{2,1,0:T(8,128)S(1)} dynamic-update-slice(f32[2,512,512]{2,1,0:T(8,128)S(1)} %get-tuple-element.333, f32[2,256,256]{2,1,0:T(8,128)S(1)} %bitcast_add_fusion.2, s32[]{:T(128)} %constant.220.clone.1..sunk, s32[]{:T(128)S(6)} %select_n.130, s32[]{:T(128)S(6)} %select_n.131) | dynamic-update-slice | bytes 1048580 | tf_op jit(solution)/shard_map/while/body/eval_jaxpr/dynamic_update_slice | solution.py:139
  167.6 2.2 %collective-permute-start.12 = (bf16[2,128,512]{2,1,0:T(8,128)(2,1)S(1)}, bf16[2,128,512]{2,1,0:T(8,128)(2,1)S(1)}, u32[]{:S(2)}, u32[]{:S(2)}) collective-permute-start(bf16[2,128,512]{2,1,0:T(8,128)(2,1)S(1)} %get-tuple-element.237), channel_id=1, source_target_pairs={{0,8},{8,16},{16,24},{1,9},{9,17},{17,25},{2,10},{10,18},{18,26},{... | collective-permute-start | bytes 786440 | tf_op jit(solution)/shard_map/ppermute | solution.py:17
  169.8 3.6 %collective-permute-start.13 = (bf16[2,128,512]{2,1,0:T(8,128)(2,1)S(1)}, bf16[2,128,512]{2,1,0:T(8,128)(2,1)S(1)}, u32[]{:S(2)}, u32[]{:S(2)}) collective-permute-start(bf16[2,128,512]{2,1,0:T(8,128)(2,1)S(1)} %get-tuple-element.238), channel_id=1, source_target_pairs={{8,0},{16,8},{24,16},{9,1},{17,9},{25,17},{10,2},{18,10},{26,18},{... | collective-permute-start | bytes 786440 | tf_op jit(solution)/shard_map/ppermute | solution.py:18
  173.6 1.7 collective-permute-done.12
  175.3 2.0 collective-permute-done.13
  178.6 1.3 collective-permute-start.14
  179.9 4.6 %collective-permute-start.15 = (bf16[2,256,128]{2,1,0:T(8,128)(2,1)S(1)}, bf16[2,256,128]{2,1,0:T(8,128)(2,1)S(1)}, u32[]{:S(2)}, u32[]{:S(2)}) collective-permute-start(bf16[2,256,128]{2,1,0:T(8,128)(2,1)S(1)} %get-tuple-element.240), channel_id=1, source_target_pairs={{1,0},{2,1},{3,2},{4,3},{5,4},{6,5},{7,6},{9,8},{10,9},{11,10},{12... | collective-permute-start | bytes 393224 | tf_op jit(solution)/shard_map/ppermute | solution.py:18
  184.5 1.5 copy.114
  186.8 5.5 %convolution_convert_fusion = bf16[8,24,16384]{2,1,0:T(8,128)(2,1)S(1)} fusion(f32[8,4,24]{2,1,0:T(4,128)S(1)} %bitcast.190, bf16[8,4,16384]{2,1,0:T(4,128)(2,1)S(1)} %reshape.183), kind=kOutput, calls=%fused_computation.5 | convolution fusion | flops 154140672 | bytes 7343104 | tf_op jit(solution)/shard_map/dpk,dpx->dkx/dot_general | solution.py:146
  193.4 1.9 collective-permute-start.16
  197.2 5.3 %collective-permute-done.16 = bf16[12,2,32,256]{3,2,1,0:T(8,128)(2,1)S(1)} collective-permute-done((bf16[12,2,32,256]{3,2,1,0:T(8,128)(2,1)S(1)}, bf16[12,2,32,256]{3,2,1,0:T(8,128)(2,1)S(1)}, u32[]{:S(2)}, u32[]{:S(2)}) %collective-permute-start.16) | collective-permute-done | bytes 393248 | tf_op jit(solution)/shard_map/ppermute | solution.py:26
  (95 shorter events, 41.4 us)
Async XLA Ops:
  1.7 47.3 %collective-permute-start.8 = (bf16[2,128,256]{2,1,0:T(8,128)(2,1)S(1)}, bf16[2,128,256]{2,1,0:T(8,128)(2,1)S(1)}, u32[]{:S(2)}, u32[]{:S(2)}) collective-permute-start(bf16[2,128,256]{2,1,0:T(8,128)(2,1)S(1)} %get-tuple-element.243), channel_id=1, source_target_pairs={{0,8},{8,16},{16,24},{1,9},{9,17},{17,25},{2,10},{10,18},{18,26},{... | collective-permute-start | bytes 393224 | tf_op jit(solution)/shard_map/ppermute | solution.py:17
  3.7 45.4 %collective-permute-start.9 = (bf16[2,128,256]{2,1,0:T(8,128)(2,1)S(1)}, bf16[2,128,256]{2,1,0:T(8,128)(2,1)S(1)}, u32[]{:S(2)}, u32[]{:S(2)}) collective-permute-start(bf16[2,128,256]{2,1,0:T(8,128)(2,1)S(1)} %get-tuple-element.244), channel_id=1, source_target_pairs={{8,0},{16,8},{24,16},{9,1},{17,9},{25,17},{10,2},{18,10},{26,18},{... | collective-permute-start | bytes 393224 | tf_op jit(solution)/shard_map/ppermute | solution.py:18
  8.9 3.7 %collective-permute-start = (f32[4,24]{0,1:T(8,128)S(1)}, f32[4,24]{0,1:T(8,128)S(1)}, u32[]{:S(2)}, u32[]{:S(2)}) collective-permute-start(f32[4,24]{0,1:T(8,128)S(1)} %copy.59), channel_id=1, source_target_pairs={{0,1},{1,2},{2,3},{3,4},{4,5},{5,6},{6,7},{7,0},{8,9},{9,10},{10,1... | collective-permute-start | bytes 1160 | tf_op jit(solution)/shard_map/ppermute | solution.py:78
  12.6 4.3 %collective-permute-start.1 = (f32[4,24]{0,1:T(8,128)S(1)}, f32[4,24]{0,1:T(8,128)S(1)}, u32[]{:S(2)}, u32[]{:S(2)}) collective-permute-start(f32[4,24]{0,1:T(8,128)S(1)} %collective-permute-done), channel_id=1, source_target_pairs={{0,1},{1,2},{2,3},{3,4},{4,5},{5,6},{6,7},{7,0},{8,9},{9,10},{10,1... | collective-permute-start | bytes 1160 | tf_op jit(solution)/shard_map/ppermute | solution.py:78
  16.9 6.4 %collective-permute-start.2 = (f32[4,24]{0,1:T(8,128)S(1)}, f32[4,24]{0,1:T(8,128)S(1)}, u32[]{:S(2)}, u32[]{:S(2)}) collective-permute-start(f32[4,24]{0,1:T(8,128)S(1)} %collective-permute-done.1), channel_id=1, source_target_pairs={{0,1},{1,2},{2,3},{3,4},{4,5},{5,6},{6,7},{7,0},{8,9},{9,10},{10,1... | collective-permute-start | bytes 1160 | tf_op jit(solution)/shard_map/ppermute | solution.py:78
  23.3 6.9 %collective-permute-start.3 = (f32[4,24]{0,1:T(8,128)S(1)}, f32[4,24]{0,1:T(8,128)S(1)}, u32[]{:S(2)}, u32[]{:S(2)}) collective-permute-start(f32[4,24]{0,1:T(8,128)S(1)} %collective-permute-done.2), channel_id=1, source_target_pairs={{0,1},{1,2},{2,3},{3,4},{4,5},{5,6},{6,7},{7,0},{8,9},{9,10},{10,1... | collective-permute-start | bytes 1160 | tf_op jit(solution)/shard_map/ppermute | solution.py:78
  28.3 27.5 %collective-permute-start.7 = (bf16[1,12,2,32,256]{4,3,2,1,0:T(8,128)(2,1)}, bf16[1,12,2,32,256]{4,3,2,1,0:T(8,128)(2,1)S(1)}, u32[]{:S(2)}, u32[]{:S(2)}) collective-permute-start(bf16[1,12,2,32,256]{4,3,2,1,0:T(8,128)(2,1)} %param.18), channel_id=1, source_target_pairs={{8,0},{16,8},{24,16},{9,1},{17,9},{25,17},{10,2},{18,10},{26,18},{... | collective-permute-start | bytes 1179656 | tf_op jit(solution)/shard_map/ppermute | solution.py:26
  30.2 5.9 %collective-permute-start.4 = (f32[4,24]{0,1:T(8,128)S(1)}, f32[4,24]{0,1:T(8,128)S(1)}, u32[]{:S(2)}, u32[]{:S(2)}) collective-permute-start(f32[4,24]{0,1:T(8,128)S(1)} %collective-permute-done.3), channel_id=1, source_target_pairs={{0,1},{1,2},{2,3},{3,4},{4,5},{5,6},{6,7},{7,0},{8,9},{9,10},{10,1... | collective-permute-start | bytes 1160 | tf_op jit(solution)/shard_map/ppermute | solution.py:78
  36.1 6.4 %collective-permute-start.5 = (f32[4,24]{0,1:T(8,128)S(1)}, f32[4,24]{0,1:T(8,128)S(1)}, u32[]{:S(2)}, u32[]{:S(2)}) collective-permute-start(f32[4,24]{0,1:T(8,128)S(1)} %collective-permute-done.4), channel_id=1, source_target_pairs={{0,1},{1,2},{2,3},{3,4},{4,5},{5,6},{6,7},{7,0},{8,9},{9,10},{10,1... | collective-permute-start | bytes 1160 | tf_op jit(solution)/shard_map/ppermute | solution.py:78
  42.5 6.4 %collective-permute-start.6 = (f32[4,24]{0,1:T(8,128)S(1)}, f32[4,24]{0,1:T(8,128)S(1)}, u32[]{:S(2)}, u32[]{:S(2)}) collective-permute-start(f32[4,24]{0,1:T(8,128)S(1)} %collective-permute-done.5), channel_id=1, source_target_pairs={{0,1},{1,2},{2,3},{3,4},{4,5},{5,6},{6,7},{7,0},{8,9},{9,10},{10,1... | collective-permute-start | bytes 1160 | tf_op jit(solution)/shard_map/ppermute | solution.py:78
  49.1 6.7 %copy-start.2 = (bf16[2,128,256]{2,1,0:T(8,128)(2,1)}, bf16[2,128,256]{2,1,0:T(8,128)(2,1)S(1)}, u32[]{:S(2)}) copy-start(bf16[2,128,256]{2,1,0:T(8,128)(2,1)S(1)} %collective-permute-done.9) | copy-start | bytes 393220
  49.2 18.0 %collective-permute-start.10 = (bf16[2,512,128]{2,1,0:T(8,128)(2,1)S(1)}, bf16[2,512,128]{2,1,0:T(8,128)(2,1)}, u32[]{:S(2)}, u32[]{:S(2)}) collective-permute-start(bf16[2,512,128]{2,1,0:T(8,128)(2,1)S(1)} %get-tuple-element.241), channel_id=1, source_target_pairs={{0,1},{1,2},{2,3},{3,4},{4,5},{5,6},{6,7},{8,9},{9,10},{10,11},{11... | collective-permute-start | bytes 786440 | tf_op jit(solution)/shard_map/ppermute | solution.py:17
  50.5 16.7 %collective-permute-start.11 = (bf16[2,512,128]{2,1,0:T(8,128)(2,1)S(1)}, bf16[2,512,128]{2,1,0:T(8,128)(2,1)}, u32[]{:S(2)}, u32[]{:S(2)}) collective-permute-start(bf16[2,512,128]{2,1,0:T(8,128)(2,1)S(1)} %get-tuple-element.242), channel_id=1, source_target_pairs={{1,0},{2,1},{3,2},{4,3},{5,4},{6,5},{7,6},{9,8},{10,9},{11,10},{12... | collective-permute-start | bytes 786440 | tf_op jit(solution)/shard_map/ppermute | solution.py:18
  57.7 7.6 %copy-start.3 = (s32[1,1,4,2]{2,3,1,0:T(2,128)S(1)}, s32[1,1,4,2]{2,3,1,0:T(2,128)}, u32[]{:S(2)}) copy-start(s32[1,1,4,2]{2,3,1,0:T(2,128)} %param.20) | copy-start | bytes 100
  59.2 22.3 %all-to-all-start = ((bf16[32,2,32,256]{3,2,1,0:T(8,128)(2,1)}), bf16[32,2,32,256]{3,2,1,0:T(8,128)(2,1)S(1)}, u32[]{:S(2)}, u32[]{:S(2)}) async-start(bf16[32,2,32,256]{3,2,1,0:T(8,128)(2,1)} %copy.63), calls=%async_computation | async-start | bytes 2097152 | tf_op jit(solution)/shard_map/all_to_all | solution.py:89
  88.3 2.6 %copy-start.4 = (bf16[1,1,4,256,256]{4,3,2,1,0:T(8,128)(2,1)S(1)}, bf16[1,1,4,256,256]{4,3,2,1,0:T(8,128)(2,1)}, u32[]{:S(2)}) copy-start(bf16[1,1,4,256,256]{4,3,2,1,0:T(8,128)(2,1)} %param.23) | copy-start | bytes 1572868
  88.4 2.6 %copy-start.5 = (f32[4]{0:T(128)S(1)}, f32[4]{0:T(128)}, u32[]{:S(2)}) copy-start(f32[4]{0:T(128)} %compare_convert_fusion) | copy-start | bytes 52
  105.7 78.8 %all-to-all-start.1 = ((bf16[4,2,256,256]{3,0,1,2:T(4,128)(2,1)}), bf16[4,2,256,256]{3,0,1,2:T(4,128)(2,1)}, u32[]{:S(2)}, u32[]{:S(2)}) async-start(bf16[4,2,256,256]{3,0,1,2:T(4,128)(2,1)} %copy.86), calls=%async_computation.1 | async-start | bytes 2097152 | tf_op jit(solution)/shard_map/all_to_all | solution.py:144
  167.6 7.7 %collective-permute-start.12 = (bf16[2,128,512]{2,1,0:T(8,128)(2,1)S(1)}, bf16[2,128,512]{2,1,0:T(8,128)(2,1)S(1)}, u32[]{:S(2)}, u32[]{:S(2)}) collective-permute-start(bf16[2,128,512]{2,1,0:T(8,128)(2,1)S(1)} %get-tuple-element.237), channel_id=1, source_target_pairs={{0,8},{8,16},{16,24},{1,9},{9,17},{17,25},{2,10},{10,18},{18,26},{... | collective-permute-start | bytes 786440 | tf_op jit(solution)/shard_map/ppermute | solution.py:17
  169.8 7.5 %collective-permute-start.13 = (bf16[2,128,512]{2,1,0:T(8,128)(2,1)S(1)}, bf16[2,128,512]{2,1,0:T(8,128)(2,1)S(1)}, u32[]{:S(2)}, u32[]{:S(2)}) collective-permute-start(bf16[2,128,512]{2,1,0:T(8,128)(2,1)S(1)} %get-tuple-element.238), channel_id=1, source_target_pairs={{8,0},{16,8},{24,16},{9,1},{17,9},{25,17},{10,2},{18,10},{26,18},{... | collective-permute-start | bytes 786440 | tf_op jit(solution)/shard_map/ppermute | solution.py:18
  177.5 1.0 copy-start
  178.6 16.7 %collective-permute-start.14 = (bf16[2,256,128]{2,1,0:T(8,128)(2,1)S(1)}, bf16[2,256,128]{2,1,0:T(8,128)(2,1)S(1)}, u32[]{:S(2)}, u32[]{:S(2)}) collective-permute-start(bf16[2,256,128]{2,1,0:T(8,128)(2,1)S(1)} %get-tuple-element.239), channel_id=1, source_target_pairs={{0,1},{1,2},{2,3},{3,4},{4,5},{5,6},{6,7},{8,9},{9,10},{10,11},{11... | collective-permute-start | bytes 393224 | tf_op jit(solution)/shard_map/ppermute | solution.py:17
  179.9 15.4 %collective-permute-start.15 = (bf16[2,256,128]{2,1,0:T(8,128)(2,1)S(1)}, bf16[2,256,128]{2,1,0:T(8,128)(2,1)S(1)}, u32[]{:S(2)}, u32[]{:S(2)}) collective-permute-start(bf16[2,256,128]{2,1,0:T(8,128)(2,1)S(1)} %get-tuple-element.240), channel_id=1, source_target_pairs={{1,0},{2,1},{3,2},{4,3},{5,4},{6,5},{7,6},{9,8},{10,9},{11,10},{12... | collective-permute-start | bytes 393224 | tf_op jit(solution)/shard_map/ppermute | solution.py:18
  193.4 9.1 %collective-permute-start.16 = (bf16[12,2,32,256]{3,2,1,0:T(8,128)(2,1)S(1)}, bf16[12,2,32,256]{3,2,1,0:T(8,128)(2,1)S(1)}, u32[]{:S(2)}, u32[]{:S(2)}) collective-permute-start(bf16[12,2,32,256]{3,2,1,0:T(8,128)(2,1)S(1)} %bitcast.189), channel_id=1, source_target_pairs={{0,8},{8,16},{16,24},{1,9},{9,17},{17,25},{2,10},{10,18},{18,26},{... | collective-permute-start | bytes 1179656 | tf_op jit(solution)/shard_map/ppermute | solution.py:26
  196.3 0.8 copy-start.1
